TPU v7x, 512 devices: a whole 4x8x8 slice. The times are simulated.
512 devices in a mesh: req: 128 (over z_hi, x, y), tp: 4 (over z_lo, core).
Axes of the slice: x: 4, y: 8, z: 8 (z_hi: 4, z_lo: 2; z = z_hi * 2 + z_lo), core: 2. Of those that a mesh axis runs over, the one named last changes fastest.
Arguments:
- queries: bfloat16 [2, 1024, 2304], P(None, 'req', 'tp'), may hold values from -10 to 10
- new_keys: bfloat16 [2, 1024, 2304], P(None, 'req', 'tp'), may hold values from -4 to 4
- new_values: bfloat16 [2, 1024, 2304], P(None, 'req', 'tp'), may hold values from -4 to 4
- cache_keys: bfloat16 [32768, 2304], P('req', 'tp'), may hold values from -10 to 10
- cache_values: bfloat16 [32768, 2304], P('req', 'tp'), may hold values from -4 to 4
- lengths: int32 [128, 16], P('req'), may hold values from 1 to 128, 256 in all within a row
- hidden: bfloat16 [2, 1024, 2304], P(None, 'req'), may hold values from -6 to 6
- gain: float32 [2304], replicated, may hold values from 0.5 to 1.5
- expert_ids: int32 [2, 1024, 2], P(None, 'req'), may hold values from 0 to 7, all different within a row; in each aligned block of 8 rows (0 to 7, 8 to 15, ..., all dimensions but the last counted through in order) at most 3 rows name the same one
- route_weights: float32 [2, 1024, 2], P(None, 'req'), may hold values from 0.2 to 1
- old_place: int32 [128], replicated, may hold values from 0 to 63, as said below
- new_place: int32 [128], replicated, may hold values from 0 to 63, as said below
- old_weights: bfloat16 [128, 2304, 1728], P('req', None, 'tp'), as said below
Outputs:
- context: bfloat16 [2, 1024, 2304], P(None, 'req', 'tp')
- layer_out: bfloat16 [2, 1024, 2304], P(None, 'req', 'tp')
- new_weights: bfloat16 [128, 2304, 1728], P('req', None, 'tp')
Inputs may be any that keep to these rules, and one draw needn't show every extreme that they name: `old_place`: every one of the 64 shards is held by at least one device; the others hold duplicates. `new_place`: every one of the 64 shards is held by at least one device; the others hold duplicates. `old_weights`: devices with equal old_place hold equal weights. `expert_ids`: in a batch, the 8 tokens of one device name one expert at most 3 times, and each token names distinct experts. `lengths`: each row sums to 256.
All inputs are finite; a program needn't handle non-finite values.
Results may differ from a plain program's by a relative error of at most 0.009.
Values may be sent and summed in bfloat16 or wider, within the bound.
A program may use at most 64 MiB of HBM per device.

v0:
```python
import jax
import jax.numpy as jnp
from jax import lax
from jax.sharding import PartitionSpec as P

HEAD_SIZE = 64
EXPERTS = 8
CAP = 3


def attend(queries, new_keys, new_values, cache_keys, cache_values, lengths):
    batches, tok_rows, width = queries.shape
    heads = width // HEAD_SIZE
    pool = cache_keys.shape[0]
    scale = HEAD_SIZE ** (-0.5)
    req_lengths = lengths.reshape(-1)
    starts = jnp.cumsum(req_lengths) - req_lengths
    position = jnp.arange(pool, dtype=jnp.int32)
    owned = (position[None, :] >= starts[:, None]) & (
        position[None, :] < (starts + req_lengths)[:, None]
    )
    query_rows = queries.reshape(batches * tok_rows, heads, HEAD_SIZE)
    own_keys = new_keys.reshape(batches * tok_rows, heads, HEAD_SIZE)
    own_values = new_values.reshape(batches * tok_rows, heads, HEAD_SIZE)
    pool_keys = cache_keys.reshape(pool, heads, HEAD_SIZE)
    pool_values = cache_values.reshape(pool, heads, HEAD_SIZE)
    scores = (
        jnp.einsum("qhd,phd->hqp", query_rows, pool_keys, preferred_element_type=jnp.float32)
        * scale
    )
    scores = jnp.where(owned[None], scores, -jnp.inf)
    own_score = (
        jnp.einsum("qhd,qhd->hq", query_rows, own_keys, preferred_element_type=jnp.float32) * scale
    )
    highest = jnp.maximum(jnp.max(scores, axis=-1), own_score)
    exp_pool = jnp.exp(scores - highest[..., None])
    exp_own = jnp.exp(own_score - highest)
    denom = jnp.sum(exp_pool, axis=-1) + exp_own
    summed = jnp.einsum(
        "hqp,phd->qhd",
        exp_pool.astype(jnp.bfloat16),
        pool_values,
        preferred_element_type=jnp.float32,
    )
    prob_own = lax.optimization_barrier(exp_own.astype(jnp.bfloat16)).astype(jnp.float32)
    summed = summed + prob_own.T[:, :, None] * own_values.astype(jnp.float32)
    context = (summed / denom.T[:, :, None]).astype(jnp.bfloat16)
    return context.reshape(batches, tok_rows, width)


def choose_holders(place, me_index, nreq, shard_count):
    devices = jnp.arange(nreq, dtype=jnp.int32)
    holder = place[None, :] == jnp.arange(shard_count, dtype=jnp.int32)[:, None]
    before = (place[:, None] == place[None, :]) & (devices[:, None] < devices[None, :])
    rank_in = jnp.sum(before.astype(jnp.int32), axis=0)
    count = jnp.sum(holder.astype(jnp.int32), axis=1)
    wanted = me_index % count
    match = holder & (rank_in[None, :] == wanted[:, None])
    return jnp.sum(jnp.where(match, devices[None, :], 0), axis=1)


def expert_block(hidden_rows, chosen, weights_now, place, shard_weights, gain):
    nreq = lax.axis_size("req")
    me_index = lax.axis_index("req")
    split_count = max(1, nreq // 16)
    shard_count = EXPERTS * split_count
    tok_rows, width = hidden_rows.shape
    hid_dev = shard_weights.shape[1] // 3
    resid = hidden_rows.astype(jnp.float32)
    normed = (
        resid * gain / jnp.sqrt(jnp.mean(resid * resid, axis=-1, keepdims=True) + 1e-05)
    ).astype(jnp.bfloat16)
    flat_ids = chosen.reshape(-1)
    assigns = flat_ids.shape[0]
    shard_dest = choose_holders(place, me_index, nreq, shard_count)
    shard_list = flat_ids[:, None] * split_count + jnp.arange(split_count, dtype=jnp.int32)[None, :]
    pick = shard_list[:, :, None] == jnp.arange(shard_count, dtype=jnp.int32)[None, None, :]
    dest = jnp.sum(jnp.where(pick, shard_dest[None, None, :], 0), axis=-1)
    assign_index = jnp.arange(assigns, dtype=jnp.int32)
    earlier = (flat_ids[:, None] == flat_ids[None, :]) & (
        assign_index[None, :] < assign_index[:, None]
    )
    rank_in = jnp.sum(earlier.astype(jnp.int32), axis=1)
    slot = dest * CAP + rank_in[:, None]
    hits = jnp.any(
        slot[None, :, :] == jnp.arange(nreq * CAP, dtype=jnp.int32)[:, None, None], axis=-1
    )
    repeated = jnp.repeat(normed, assigns // tok_rows, axis=0)
    outgoing = jnp.dot(hits.astype(jnp.bfloat16), repeated, preferred_element_type=jnp.float32)
    outgoing = outgoing.astype(jnp.bfloat16).reshape(nreq, CAP, width)
    received = lax.all_to_all(outgoing, "req", split_axis=0, concat_axis=0, tiled=True)
    sources, items, feat = received.shape
    flat_rows = received.reshape(sources * items, feat)
    gate_up = jnp.dot(
        flat_rows, shard_weights[:, : 2 * hid_dev], preferred_element_type=jnp.float32
    )
    act = (jax.nn.silu(gate_up[:, :hid_dev]) * gate_up[:, hid_dev:]).astype(jnp.bfloat16)
    part = lax.dot_general(
        act,
        shard_weights[:, 2 * hid_dev :],
        (((1,), (1,)), ((), ())),
        preferred_element_type=jnp.float32,
    )
    part = part.astype(jnp.bfloat16).reshape(sources, items, feat)
    returned = lax.all_to_all(part, "req", split_axis=0, concat_axis=0, tiled=True)
    returned = returned.reshape(nreq * CAP, width)
    picked = (
        returned[slot.reshape(-1)]
        .astype(jnp.float32)
        .reshape(tok_rows, assigns // tok_rows, split_count, width)
    )
    partial_sum = jnp.einsum("rksd,rk->rd", picked, weights_now)
    tp_width = width // lax.axis_size("tp")
    tp_start = lax.axis_index("tp") * tp_width
    resid_share = lax.dynamic_slice_in_dim(resid, tp_start, tp_width, 1)
    whole = lax.psum(partial_sum.astype(jnp.bfloat16), "tp").astype(jnp.float32)
    share = lax.dynamic_slice_in_dim(whole, tp_start, tp_width, 1)
    return (resid_share + share).astype(jnp.bfloat16)


def migrate(old_weights, old_place, new_place):
    nreq = lax.axis_size("req")
    shard_count = EXPERTS * max(1, nreq // 16)
    _, width, columns = old_weights.shape
    piece = width // nreq
    pieces = old_weights.reshape(nreq, piece, columns)
    spread = lax.all_to_all(pieces, "req", split_axis=0, concat_axis=0, tiled=True)
    devices = jnp.arange(nreq, dtype=jnp.int32)
    shard_ids = jnp.arange(shard_count, dtype=jnp.int32)
    first_old = jnp.min(
        jnp.where(old_place[None, :] == shard_ids[:, None], devices[None, :], nreq), axis=1
    )
    needed = jnp.sum(
        jnp.where(new_place[:, None] == shard_ids[None, :], first_old[None, :], 0), axis=1
    )
    sending = spread[needed]
    collected = lax.all_to_all(sending, "req", split_axis=0, concat_axis=0, tiled=True)
    return collected.reshape(1, width, columns)


def on_device(
    queries,
    new_keys,
    new_values,
    cache_keys,
    cache_values,
    lengths,
    hidden,
    gain,
    expert_ids,
    route_weights,
    old_place,
    new_place,
    old_weights,
):
    context = attend(queries, new_keys, new_values, cache_keys, cache_values, lengths)
    moved = migrate(old_weights, old_place, new_place)
    first_out = expert_block(
        hidden[0], expert_ids[0], route_weights[0], old_place, old_weights[0], gain
    )
    second_out = expert_block(hidden[1], expert_ids[1], route_weights[1], new_place, moved[0], gain)
    layer_out = jnp.stack([first_out, second_out])
    return (context, layer_out, moved)


def solution(mesh):
    in_specs = (
        P(None, "req", "tp"),
        P(None, "req", "tp"),
        P(None, "req", "tp"),
        P("req", "tp"),
        P("req", "tp"),
        P("req", None),
        P(None, "req", None),
        P(),
        P(None, "req", None),
        P(None, "req", None),
        P(),
        P(),
        P("req", None, "tp"),
    )
    out_specs = (P(None, "req", "tp"), P(None, "req", "tp"), P("req", None, "tp"))
    return jax.shard_map(
        on_device, mesh=mesh, in_specs=in_specs, out_specs=out_specs, check_vma=False
    )
```

profile of v0, /device:TPU:1, one launch (start us, length us, event | category | flops | bytes accessed | tf_op | source)
XLA Modules:
  0.0 525.8 jit_solution(8682452073270853563)
XLA Ops:
  7.2 0.8 convert_reduce_fusion.4
  8.0 0.8 convert_reduce_fusion.2
  8.8 0.7 fusion.48
  9.9 0.9 fusion.27
  10.9 0.9 fusion.26
  11.9 0.8 convert_reduce_fusion.5
  12.8 0.8 select_reduce_fusion.4
  14.3 0.7 convolution_convert_fusion
  15.0 2.3 reshape.378
  17.2 20.8 %all-to-all-start.2 = ((bf16[128,3,2304]{2,1,0:T(4,128)(2,1)}), bf16[128,3,2304]{2,1,0:T(4,128)(2,1)S(1)}, u32[]{:S(2)}, u32[]{:S(2)}) async-start(bf16[128,3,2304]{2,1,0:T(4,128)(2,1)} %reshape.378), calls=%async_computation.2 | async-start | bytes 4718592 | tf_op jit(solution)/shard_map/all_to_all | solution.py:91
  38.1 4.1 copy.34
  42.1 5.2 reshape.380
  47.4 49.8 %all-to-all-done.2 = bf16[128,3,2304]{2,1,0:T(4,128)(2,1)S(1)} async-done(((bf16[128,3,2304]{2,1,0:T(4,128)(2,1)}), bf16[128,3,2304]{2,1,0:T(4,128)(2,1)S(1)}, u32[]{:S(2)}, u32[]{:S(2)}) %all-to-all-start.2) | async-done | bytes 1769504 | tf_op jit(solution)/shard_map/all_to_all | solution.py:91
  97.2 1.4 copy-done.1
  98.6 7.6 %all-to-all-start.3 = ((bf16[128,18,432]{2,1,0:T(8,128)(2,1)}), bf16[128,18,432]{2,1,0:T(8,128)(2,1)S(1)}, u32[]{:S(2)}, u32[]{:S(2)}) async-start(bf16[128,18,432]{2,1,0:T(8,128)(2,1)} %reshape.380), calls=%async_computation.3 | async-start | bytes 6291456 | tf_op jit(solution)/shard_map/all_to_all | solution.py:127
  106.4 0.7 broadcast_in_dim.84
  107.0 0.9 reshape.372
  109.1 1.9 convolution_convert_fusion.2
  111.0 5.4 %reshape.373 = bf16[128,3,2304]{2,1,0:T(4,128)(2,1)} reshape(bf16[384,2304]{1,0:T(8,128)(2,1)} %convolution_convert_fusion.2) | data formatting | bytes 3538944 | tf_op jit(solution)/shard_map/reshape | solution.py:90
  116.4 64.4 %all-to-all-done.3 = bf16[128,18,432]{2,1,0:T(8,128)(2,1)S(1)} async-done(((bf16[128,18,432]{2,1,0:T(8,128)(2,1)}), bf16[128,18,432]{2,1,0:T(8,128)(2,1)S(1)}, u32[]{:S(2)}, u32[]{:S(2)}) %all-to-all-start.3) | async-done | bytes 1990688 | tf_op jit(solution)/shard_map/all_to_all | solution.py:127
  180.8 8.4 %all-to-all-start = ((bf16[128,3,2304]{2,1,0:T(4,128)(2,1)}), bf16[128,3,2304]{2,1,0:T(4,128)(2,1)}, u32[]{:S(2)}, u32[]{:S(2)}) async-start(bf16[128,3,2304]{2,1,0:T(4,128)(2,1)} %reshape.373), calls=%async_computation | async-start | bytes 4718592 | tf_op jit(solution)/shard_map/all_to_all | solution.py:91
  189.3 2.4 gather_fusion.1
  191.7 53.7 %all-to-all-done = bf16[128,3,2304]{2,1,0:T(4,128)(2,1)} async-done(((bf16[128,3,2304]{2,1,0:T(4,128)(2,1)}), bf16[128,3,2304]{2,1,0:T(4,128)(2,1)}, u32[]{:S(2)}, u32[]{:S(2)}) %all-to-all-start) | async-done | bytes 1769504 | tf_op jit(solution)/shard_map/all_to_all | solution.py:91
  245.4 7.3 %all-to-all-start.4 = ((bf16[128,18,432]{2,1,0:T(8,128)(2,1)}), bf16[128,18,432]{2,1,0:T(8,128)(2,1)S(1)}, u32[]{:S(2)}, u32[]{:S(2)}) async-start(bf16[128,18,432]{2,1,0:T(8,128)(2,1)} %gather_fusion.1), calls=%async_computation.4 | async-start | bytes 6291456 | tf_op jit(solution)/shard_map/all_to_all | solution.py:137
  252.7 5.2 reshape.374
  257.9 2.7 fusion.2
  260.6 3.0 convolution_convert_fusion.1
  263.6 5.3 %reshape.375 = bf16[128,3,2304]{2,1,0:T(4,128)(2,1)} reshape(bf16[384,2304]{1,0:T(8,128)(2,1)} %convolution_convert_fusion.1) | data formatting | bytes 3538944 | tf_op jit(solution)/shard_map/reshape | solution.py:104
  269.0 55.9 %all-to-all-done.4 = bf16[128,18,432]{2,1,0:T(8,128)(2,1)S(1)} async-done(((bf16[128,18,432]{2,1,0:T(8,128)(2,1)}), bf16[128,18,432]{2,1,0:T(8,128)(2,1)S(1)}, u32[]{:S(2)}, u32[]{:S(2)}) %all-to-all-start.4) | async-done | bytes 1990688 | tf_op jit(solution)/shard_map/all_to_all | solution.py:137
  324.9 8.0 %all-to-all-start.1 = ((bf16[128,3,2304]{2,1,0:T(4,128)(2,1)}), bf16[128,3,2304]{2,1,0:T(4,128)(2,1)}, u32[]{:S(2)}, u32[]{:S(2)}) async-start(bf16[128,3,2304]{2,1,0:T(4,128)(2,1)} %reshape.375), calls=%async_computation.1 | async-start | bytes 4718592 | tf_op jit(solution)/shard_map/all_to_all | solution.py:105
  334.1 5.2 reshape.379
  339.2 2.6 squeeze_reshape.3
  341.8 3.1 fusion
  344.9 2.3 convolution_convert_fusion.3
  347.2 5.3 %reshape.381 = bf16[128,3,2304]{2,1,0:T(4,128)(2,1)} reshape(bf16[384,2304]{1,0:T(8,128)(2,1)} %convolution_convert_fusion.3) | data formatting | bytes 3538944 | tf_op jit(solution)/shard_map/reshape | solution.py:104
  352.6 33.7 %all-to-all-done.1 = bf16[128,3,2304]{2,1,0:T(4,128)(2,1)} async-done(((bf16[128,3,2304]{2,1,0:T(4,128)(2,1)}), bf16[128,3,2304]{2,1,0:T(4,128)(2,1)}, u32[]{:S(2)}, u32[]{:S(2)}) %all-to-all-start.1) | async-done | bytes 1769504 | tf_op jit(solution)/shard_map/all_to_all | solution.py:105
  386.3 7.9 %all-to-all-start.5 = ((bf16[128,3,2304]{2,1,0:T(4,128)(2,1)}), bf16[128,3,2304]{2,1,0:T(4,128)(2,1)}, u32[]{:S(2)}, u32[]{:S(2)}) async-start(bf16[128,3,2304]{2,1,0:T(4,128)(2,1)} %reshape.381), calls=%async_computation.5 | async-start | bytes 4718592 | tf_op jit(solution)/shard_map/all_to_all | solution.py:105
  394.5 0.7 copy.45
  395.2 0.7 copy.43
  396.1 0.7 reshape.367
  396.8 1.4 reshape.369
  398.3 1.0 fusion.14
  399.4 0.7 bitcast_subtract_fusion
  400.1 1.7 fusion.49
  401.8 1.5 reshape.384
  403.2 0.7 fusion.45
  403.9 0.7 fusion.43
  405.2 1.1 fusion.15
  407.5 0.7 slice_convert_fusion.1
  408.1 5.2 reshape.376
  413.3 4.2 gather_fusion
  417.5 1.5 convert_reduce_fusion.1
  419.9 26.4 %all-to-all-done.5 = bf16[128,3,2304]{2,1,0:T(4,128)(2,1)} async-done(((bf16[128,3,2304]{2,1,0:T(4,128)(2,1)}), bf16[128,3,2304]{2,1,0:T(4,128)(2,1)}, u32[]{:S(2)}, u32[]{:S(2)}) %all-to-all-start.5) | async-done | bytes 1769504 | tf_op jit(solution)/shard_map/all_to_all | solution.py:105
  446.3 5.2 reshape.382
  451.5 4.1 gather_fusion.2
  455.7 1.5 convert_reduce_fusion
  458.1 1.3 fusion.8
  459.5 0.7 reshape.371
  460.2 2.6 reshape.383
  462.8 4.1 copy.35
  466.9 49.8 %all-reduce.3.cloned.1.call-done = (bf16[8,2304]{1,0:T(8,128)(2,1)}, bf16[8,2304]{1,0:T(8,128)(2,1)}) async-done(((bf16[8,2304]{1,0:T(8,128)(2,1)}, bf16[8,2304]{1,0:T(8,128)(2,1)}), (bf16[8,2304]{1,0:T(8,128)(2,1)}, bf16[8,2304]{1,0:T(8,128)(2,1)})) %all-reduce.3.cloned.1.call-update) | async-done | bytes 73744 | tf_op jit(solution)/shard_map/psum | solution.py:116
  516.7 0.8 fusion.37
  517.5 0.8 fusion.38
  518.3 0.6 pad_maximum_fusion
  (70 shorter events, 8.2 us)
Async XLA Ops:
  7.2 392.9 %copy-start = (bf16[256,576]{0,1:T(8,128)(2,1)S(1)}, bf16[256,576]{0,1:T(8,128)(2,1)}, u32[]{:S(2)}) copy-start(bf16[256,576]{0,1:T(8,128)(2,1)} %param.16) | copy-start | bytes 884740
  17.2 79.9 %all-to-all-start.2 = ((bf16[128,3,2304]{2,1,0:T(4,128)(2,1)}), bf16[128,3,2304]{2,1,0:T(4,128)(2,1)S(1)}, u32[]{:S(2)}, u32[]{:S(2)}) async-start(bf16[128,3,2304]{2,1,0:T(4,128)(2,1)} %reshape.378), calls=%async_computation.2 | async-start | bytes 4718592 | tf_op jit(solution)/shard_map/all_to_all | solution.py:91
  47.4 60.8 %copy-start.9 = (s32[128]{0:T(128)S(1)}, s32[128]{0:T(128)}, u32[]{:S(2)}) copy-start(s32[128]{0:T(128)} %param.23) | copy-start | bytes 1540
  97.2 1.4 copy-start.1
  98.6 82.2 %all-to-all-start.3 = ((bf16[128,18,432]{2,1,0:T(8,128)(2,1)}), bf16[128,18,432]{2,1,0:T(8,128)(2,1)S(1)}, u32[]{:S(2)}, u32[]{:S(2)}) async-start(bf16[128,18,432]{2,1,0:T(8,128)(2,1)} %reshape.380), calls=%async_computation.3 | async-start | bytes 6291456 | tf_op jit(solution)/shard_map/all_to_all | solution.py:127
  116.4 72.8 %copy-start.12 = (s32[128]{0:T(128)S(1)}, s32[128]{0:T(128)}, u32[]{:S(2)}) copy-start(s32[128]{0:T(128)} %param.24) | copy-start | bytes 1540
  180.8 64.7 %all-to-all-start = ((bf16[128,3,2304]{2,1,0:T(4,128)(2,1)}), bf16[128,3,2304]{2,1,0:T(4,128)(2,1)}, u32[]{:S(2)}, u32[]{:S(2)}) async-start(bf16[128,3,2304]{2,1,0:T(4,128)(2,1)} %reshape.373), calls=%async_computation | async-start | bytes 4718592 | tf_op jit(solution)/shard_map/all_to_all | solution.py:91
  245.4 79.4 %all-to-all-start.4 = ((bf16[128,18,432]{2,1,0:T(8,128)(2,1)}), bf16[128,18,432]{2,1,0:T(8,128)(2,1)S(1)}, u32[]{:S(2)}, u32[]{:S(2)}) async-start(bf16[128,18,432]{2,1,0:T(8,128)(2,1)} %gather_fusion.1), calls=%async_computation.4 | async-start | bytes 6291456 | tf_op jit(solution)/shard_map/all_to_all | solution.py:137
  324.9 61.4 %all-to-all-start.1 = ((bf16[128,3,2304]{2,1,0:T(4,128)(2,1)}), bf16[128,3,2304]{2,1,0:T(4,128)(2,1)}, u32[]{:S(2)}, u32[]{:S(2)}) async-start(bf16[128,3,2304]{2,1,0:T(4,128)(2,1)} %reshape.375), calls=%async_computation.1 | async-start | bytes 4718592 | tf_op jit(solution)/shard_map/all_to_all | solution.py:105
  341.8 3.1 copy-start.2
  352.6 41.9 %copy-start.11 = (f32[2,8,2]{1,2,0:T(2,128)S(1)}, f32[2,8,2]{1,2,0:T(2,128)}, u32[]{:S(2)}) copy-start(f32[2,8,2]{1,2,0:T(2,128)} %param.22) | copy-start | bytes 388
  352.6 43.3 %copy-start.10 = (s32[1,16]{1,0:T(1,128)S(1)}, s32[1,16]{1,0:T(1,128)}, u32[]{:S(2)}) copy-start(s32[1,16]{1,0:T(1,128)} %param.18) | copy-start | bytes 196
  352.6 43.5 %copy-start.4 = (bf16[2,8,576]{2,1,0:T(8,128)(2,1)S(1)}, bf16[2,8,576]{2,1,0:T(8,128)(2,1)}, u32[]{:S(2)}) copy-start(bf16[2,8,576]{2,1,0:T(8,128)(2,1)} %param.13) | copy-start | bytes 55300
  352.6 54.9 %copy-start.3 = (bf16[2,8,2304]{2,1,0:T(8,128)(2,1)S(1)}, bf16[2,8,2304]{2,1,0:T(8,128)(2,1)}, u32[]{:S(2)}) copy-start(bf16[2,8,2304]{2,1,0:T(8,128)(2,1)} %param.19) | copy-start | bytes 221188
  386.3 60.0 %all-to-all-start.5 = ((bf16[128,3,2304]{2,1,0:T(4,128)(2,1)}), bf16[128,3,2304]{2,1,0:T(4,128)(2,1)}, u32[]{:S(2)}, u32[]{:S(2)}) async-start(bf16[128,3,2304]{2,1,0:T(4,128)(2,1)} %reshape.381), calls=%async_computation.5 | async-start | bytes 4718592 | tf_op jit(solution)/shard_map/all_to_all | solution.py:105
  394.2 122.5 %all-reduce.3.cloned.1.call-start = ((), (), s32[]{:S(2)}) async-start(), calls=%async_computation.6 | async-start | bytes 147456 | tf_op jit(solution)/shard_map/psum | solution.py:116
  413.3 5.7 %copy-start.8 = (bf16[8,2,1]{1,2,0:T(2,128)(2,1)S(1)}, bf16[8,2,1]{1,2,0:T(2,128)(2,1)}, u32[]{:S(2)}) copy-start(bf16[8,2,1]{1,2,0:T(2,128)(2,1)} %copy.43) | copy-start | bytes 100
  451.5 5.7 %copy-start.7 = (bf16[8,2,1]{1,2,0:T(2,128)(2,1)S(1)}, bf16[8,2,1]{1,2,0:T(2,128)(2,1)}, u32[]{:S(2)}) copy-start(bf16[8,2,1]{1,2,0:T(2,128)(2,1)} %copy.45) | copy-start | bytes 100
  451.5 6.5 %copy-start.5 = (f32[16,9]{0,1:T(8,128)S(1)}, f32[16,9]{0,1:T(8,128)}, u32[]{:S(2)}) copy-start(f32[16,9]{0,1:T(8,128)} %convert_bitcast_fusion) | copy-start | bytes 1732
  451.5 6.6 %copy-start.6 = (f32[16,9]{0,1:T(8,128)S(1)}, f32[16,9]{0,1:T(8,128)}, u32[]{:S(2)}) copy-start(f32[16,9]{0,1:T(8,128)} %fusion.40) | copy-start | bytes 1732
Sparse Core Ops, SparseCore 0:
  458.2 58.4 all-reduce.2
where the time goes:
time: 528 us; the launch traced here: 526 us
  waiting for transfers between devices  334 us (63%)
  local copies, waits for them, and re-layouts  81 us (15%)
  starting transfers between devices  60.2 us (11%)
  other arithmetic  19.5 us (4%)
  matrix products  17 us (3%)
  between operations  14.3 us (3%)
    all_to_all x2, waiting for transfers between devices, expert_block(): lax.all_to_all(outgoing, 'req', split_axis=0, concat_axis=0, tiled=True)  104 us
    all_to_all x1, waiting for transfers between devices, migrate(): lax.all_to_all(pieces, 'req', split_axis=0, concat_axis=0, tiled=True)  64.4 us
    all_to_all x2, waiting for transfers between devices, expert_block(): lax.all_to_all(part, 'req', split_axis=0, concat_axis=0, tiled=True)  60.1 us
    all_to_all x1, waiting for transfers between devices, migrate(): lax.all_to_all(sending, 'req', split_axis=0, concat_axis=0, tiled=True)  55.9 us
    psum x1, waiting for transfers between devices, expert_block(): whole = lax.psum(partial_sum.astype(jnp.bfloat16), 'tp').astype(jnp.float32)  49.8 us
    all_to_all x2, starting transfers between devices, expert_block(): lax.all_to_all(outgoing, 'req', split_axis=0, concat_axis=0, tiled=True)  29.2 us
    all_to_all x2, starting transfers between devices, expert_block(): lax.all_to_all(part, 'req', split_axis=0, concat_axis=0, tiled=True)  15.9 us
    reshape x2, local copies, waits for them, and re-layouts, expert_block(): part = part.astype(jnp.bfloat16).reshape(sources, items, feat)  10.7 us
  transfers between devices with their start and end apart: 7, of which 7 were waited for; matrix products, arithmetic and copies ran while one was open for 18% of the time, Pallas kernels for 0%

commit v1 on v0

--- a/solution.py
+++ b/solution.py
@@ -113,7 +113,9 @@
     tp_width = width // lax.axis_size("tp")
     tp_start = lax.axis_index("tp") * tp_width
     resid_share = lax.dynamic_slice_in_dim(resid, tp_start, tp_width, 1)
-    whole = lax.psum(partial_sum.astype(jnp.bfloat16), "tp").astype(jnp.float32)
+    whole = jnp.sum(lax.all_gather(partial_sum.astype(jnp.bfloat16), axis_name="tp"), 0).astype(
+        jnp.float32
+    )
     share = lax.dynamic_slice_in_dim(whole, tp_start, tp_width, 1)
     return (resid_share + share).astype(jnp.bfloat16)
 

time: 528 us -> 477 us (0.903)
  waiting for transfers between devices: 334 us -> 261 us
  blocking collectives: 0 us -> 43.5 us
  between operations: 14.3 us -> 0.95 us
  local copies, waits for them, and re-layouts: 81 us -> 74.9 us
    psum x1 -> x0, waiting for transfers between devices: 49.8 us -> none  [expert_block(): whole = lax.psum(partial_sum.astype(jnp.bfloat16), 'tp').astype(jnp.float32)]
    all_gather x0 -> x2, blocking collectives: none -> 43.5 us  [expert_block(): lax.all_gather(partial_sum.astype(jnp.bfloat16), axis_name='tp')]
    all_to_all x2, waiting for transfers between devices: 60.1 us -> 34.1 us  [expert_block(): lax.all_to_all(part, 'req', split_axis=0, concat_axis=0, tiled=True)]
  transfers between devices with their start and end apart: 7 -> 6, of which waited for: 7 -> 5; matrix products, arithmetic and copies ran while one was open for 18% -> 19% of each run, Pallas kernels for 0% -> 0%
where the time goes in v1:
time: 477 us; the launch traced here: 475 us
  waiting for transfers between devices  261 us (55%)
  local copies, waits for them, and re-layouts  74.9 us (16%)
  starting transfers between devices  60.4 us (13%)
  blocking collectives  43.5 us (9%)
  other arithmetic  17.1 us (4%)
  matrix products  17 us (4%)
    all_to_all x2, waiting for transfers between devices, expert_block(): lax.all_to_all(outgoing, 'req', split_axis=0, concat_axis=0, tiled=True)  104 us
    all_to_all x1, waiting for transfers between devices, migrate(): lax.all_to_all(pieces, 'req', split_axis=0, concat_axis=0, tiled=True)  65 us
    all_to_all x1, waiting for transfers between devices, migrate(): lax.all_to_all(sending, 'req', split_axis=0, concat_axis=0, tiled=True)  58 us
    all_gather x2, blocking collectives, expert_block(): lax.all_gather(partial_sum.astype(jnp.bfloat16), axis_name='tp')  43.5 us
    all_to_all x2, waiting for transfers between devices, expert_block(): lax.all_to_all(part, 'req', split_axis=0, concat_axis=0, tiled=True)  34.1 us
    all_to_all x2, starting transfers between devices, expert_block(): lax.all_to_all(outgoing, 'req', split_axis=0, concat_axis=0, tiled=True)  29 us
    all_to_all x2, starting transfers between devices, expert_block(): lax.all_to_all(part, 'req', split_axis=0, concat_axis=0, tiled=True)  15.5 us
    reshape x2, local copies, waits for them, and re-layouts, expert_block(): part = part.astype(jnp.bfloat16).reshape(sources, items, feat)  10.7 us
  transfers between devices with their start and end apart: 6, of which 5 were waited for; matrix products, arithmetic and copies ran while one was open for 19% of the time, Pallas kernels for 0%

profile of v1, /device:TPU:1, one launch (start us, length us, event | category | flops | bytes accessed | tf_op | source)
XLA Modules:
  0.0 475.0 jit_solution(3200980609622334973)
XLA Ops:
  0.6 0.8 convert_reduce_fusion.4
  1.5 0.8 convert_reduce_fusion.2
  2.3 0.7 fusion.48
  3.3 0.9 fusion.27
  4.3 0.9 fusion.26
  5.4 0.8 convert_reduce_fusion.5
  6.3 0.8 select_reduce_fusion.4
  7.8 0.7 convolution_convert_fusion
  8.4 2.3 reshape.378
  10.7 20.8 %all-to-all-start.2 = ((bf16[128,3,2304]{2,1,0:T(4,128)(2,1)}), bf16[128,3,2304]{2,1,0:T(4,128)(2,1)S(1)}, u32[]{:S(2)}, u32[]{:S(2)}) async-start(bf16[128,3,2304]{2,1,0:T(4,128)(2,1)} %reshape.378), calls=%async_computation.2 | async-start | bytes 4718592 | tf_op jit(solution)/shard_map/all_to_all | solution.py:91
  31.5 4.1 copy.34
  35.6 5.2 %reshape.380 = bf16[128,18,432]{2,1,0:T(8,128)(2,1)} reshape(bf16[1,2304,432]{2,1,0:T(8,128)(2,1)} %copy.34) | data formatting | bytes 3981312 | tf_op jit(solution)/shard_map/reshape | solution.py:128
  40.8 49.8 %all-to-all-done.2 = bf16[128,3,2304]{2,1,0:T(4,128)(2,1)S(1)} async-done(((bf16[128,3,2304]{2,1,0:T(4,128)(2,1)}), bf16[128,3,2304]{2,1,0:T(4,128)(2,1)S(1)}, u32[]{:S(2)}, u32[]{:S(2)}) %all-to-all-start.2) | async-done | bytes 1769504 | tf_op jit(solution)/shard_map/all_to_all | solution.py:91
  90.6 1.4 copy-done.1
  92.1 7.6 %all-to-all-start.3 = ((bf16[128,18,432]{2,1,0:T(8,128)(2,1)}), bf16[128,18,432]{2,1,0:T(8,128)(2,1)S(1)}, u32[]{:S(2)}, u32[]{:S(2)}) async-start(bf16[128,18,432]{2,1,0:T(8,128)(2,1)} %reshape.380), calls=%async_computation.3 | async-start | bytes 6291456 | tf_op jit(solution)/shard_map/all_to_all | solution.py:129
  99.8 0.7 broadcast_in_dim.84
  100.5 0.9 reshape.372
  102.6 1.9 convolution_convert_fusion.2
  104.5 5.4 %reshape.373 = bf16[128,3,2304]{2,1,0:T(4,128)(2,1)} reshape(bf16[384,2304]{1,0:T(8,128)(2,1)} %convolution_convert_fusion.2) | data formatting | bytes 3538944 | tf_op jit(solution)/shard_map/reshape | solution.py:90
  109.9 65.0 %all-to-all-done.3 = bf16[128,18,432]{2,1,0:T(8,128)(2,1)S(1)} async-done(((bf16[128,18,432]{2,1,0:T(8,128)(2,1)}), bf16[128,18,432]{2,1,0:T(8,128)(2,1)S(1)}, u32[]{:S(2)}, u32[]{:S(2)}) %all-to-all-start.3) | async-done | bytes 1990688 | tf_op jit(solution)/shard_map/all_to_all | solution.py:129
  174.9 8.2 %all-to-all-start = ((bf16[128,3,2304]{2,1,0:T(4,128)(2,1)}), bf16[128,3,2304]{2,1,0:T(4,128)(2,1)}, u32[]{:S(2)}, u32[]{:S(2)}) async-start(bf16[128,3,2304]{2,1,0:T(4,128)(2,1)} %reshape.373), calls=%async_computation | async-start | bytes 4718592 | tf_op jit(solution)/shard_map/all_to_all | solution.py:91
  183.2 2.4 gather_fusion.1
  185.6 54.2 %all-to-all-done = bf16[128,3,2304]{2,1,0:T(4,128)(2,1)} async-done(((bf16[128,3,2304]{2,1,0:T(4,128)(2,1)}), bf16[128,3,2304]{2,1,0:T(4,128)(2,1)}, u32[]{:S(2)}, u32[]{:S(2)}) %all-to-all-start) | async-done | bytes 1769504 | tf_op jit(solution)/shard_map/all_to_all | solution.py:91
  239.8 8.3 %all-to-all-start.4 = ((bf16[128,18,432]{2,1,0:T(8,128)(2,1)}), bf16[128,18,432]{2,1,0:T(8,128)(2,1)S(1)}, u32[]{:S(2)}, u32[]{:S(2)}) async-start(bf16[128,18,432]{2,1,0:T(8,128)(2,1)} %gather_fusion.1), calls=%async_computation.4 | async-start | bytes 6291456 | tf_op jit(solution)/shard_map/all_to_all | solution.py:139
  248.2 5.2 %reshape.374 = bf16[384,2304]{1,0:T(8,128)(2,1)} reshape(bf16[128,3,2304]{2,1,0:T(4,128)(2,1)} %all-to-all-done) | data formatting | bytes 3538944 | tf_op jit(solution)/shard_map/reshape | solution.py:93
  253.4 2.7 fusion.2
  256.1 3.0 convolution_convert_fusion.1
  259.1 5.4 %reshape.375 = bf16[128,3,2304]{2,1,0:T(4,128)(2,1)} reshape(bf16[384,2304]{1,0:T(8,128)(2,1)} %convolution_convert_fusion.1) | data formatting | bytes 3538944 | tf_op jit(solution)/shard_map/reshape | solution.py:104
  264.4 58.0 %all-to-all-done.4 = bf16[128,18,432]{2,1,0:T(8,128)(2,1)S(1)} async-done(((bf16[128,18,432]{2,1,0:T(8,128)(2,1)}), bf16[128,18,432]{2,1,0:T(8,128)(2,1)S(1)}, u32[]{:S(2)}, u32[]{:S(2)}) %all-to-all-start.4) | async-done | bytes 1990688 | tf_op jit(solution)/shard_map/all_to_all | solution.py:139
  322.5 7.8 %all-to-all-start.1 = ((bf16[128,3,2304]{2,1,0:T(4,128)(2,1)}), bf16[128,3,2304]{2,1,0:T(4,128)(2,1)}, u32[]{:S(2)}, u32[]{:S(2)}) async-start(bf16[128,3,2304]{2,1,0:T(4,128)(2,1)} %reshape.375), calls=%async_computation.1 | async-start | bytes 4718592 | tf_op jit(solution)/shard_map/all_to_all | solution.py:105
  330.5 0.7 reshape.367
  331.3 0.7 reshape.369
  332.5 5.2 %reshape.379 = bf16[384,2304]{1,0:T(8,128)(2,1)} reshape(bf16[128,3,2304]{2,1,0:T(4,128)(2,1)} %copy-done.1) | data formatting | bytes 3538944 | tf_op jit(solution)/shard_map/reshape | solution.py:93
  337.7 2.6 squeeze_reshape.3
  340.3 3.1 fusion
  343.4 2.3 convolution_convert_fusion.3
  345.7 5.3 %reshape.381 = bf16[128,3,2304]{2,1,0:T(4,128)(2,1)} reshape(bf16[384,2304]{1,0:T(8,128)(2,1)} %convolution_convert_fusion.3) | data formatting | bytes 3538944 | tf_op jit(solution)/shard_map/reshape | solution.py:104
  351.0 34.1 %all-to-all-done.1 = bf16[128,3,2304]{2,1,0:T(4,128)(2,1)} async-done(((bf16[128,3,2304]{2,1,0:T(4,128)(2,1)}), bf16[128,3,2304]{2,1,0:T(4,128)(2,1)}, u32[]{:S(2)}, u32[]{:S(2)}) %all-to-all-start.1) | async-done | bytes 1769504 | tf_op jit(solution)/shard_map/all_to_all | solution.py:105
  385.1 7.7 %all-to-all-start.5 = ((bf16[128,3,2304]{2,1,0:T(4,128)(2,1)}), bf16[128,3,2304]{2,1,0:T(4,128)(2,1)}, u32[]{:S(2)}, u32[]{:S(2)}) async-start(bf16[128,3,2304]{2,1,0:T(4,128)(2,1)} %reshape.381), calls=%async_computation.5 | async-start | bytes 4718592 | tf_op jit(solution)/shard_map/all_to_all | solution.py:105
  392.8 1.0 fusion.14
  393.8 0.6 add.195
  394.4 0.7 add.182
  395.3 0.7 fusion.36
  396.0 1.7 fusion.49
  397.7 1.5 reshape.384
  399.2 1.1 fusion.15
  400.3 1.3 fusion.8
  401.6 0.7 copy.31
  402.3 1.5 reshape.371
  403.8 0.6 fusion.45
  404.4 0.7 fusion.43
  405.1 0.7 slice_convert_fusion.1
  405.7 5.2 %reshape.376 = bf16[384,2304]{1,0:T(8,128)(2,1)} reshape(bf16[128,3,2304]{2,1,0:T(4,128)(2,1)} %all-to-all-done.1) | data formatting | bytes 3538944 | tf_op jit(solution)/shard_map/reshape | solution.py:106
  410.9 4.1 gather_fusion
  415.0 1.5 convert_reduce_fusion.1
  416.8 32.7 %all-gather = bf16[32,2304]{1,0:T(8,128)(2,1)S(1)} all-gather(bf16[8,2304]{1,0:T(8,128)(2,1)S(1)} %bitcast.105), channel_id=2, replica_groups=mesh['req'=128,'tp'=4] {'tp'}, dimensions={0}, use_global_device_ids=true | all-gather | bytes 184320 | tf_op jit(solution)/shard_map/all_gather | solution.py:116
  449.5 0.8 fusion.37
  450.3 2.6 reshape.383
  452.9 4.1 copy.35
  457.0 4.1 reshape.382
  461.1 1.0 gather_fusion.2
  462.8 10.8 %all-gather.1 = bf16[32,2304]{1,0:T(8,128)(2,1)S(1)} all-gather(bf16[8,2304]{1,0:T(8,128)(2,1)S(1)} %bitcast.106), channel_id=3, replica_groups=mesh['req'=128,'tp'=4] {'tp'}, dimensions={0}, use_global_device_ids=true | all-gather | bytes 184320 | tf_op jit(solution)/shard_map/all_gather | solution.py:116
  473.6 0.8 fusion.38
  474.4 0.6 pad_maximum_fusion
  (65 shorter events, 4.8 us)
Async XLA Ops:
  0.6 395.4 %copy-start = (bf16[256,576]{0,1:T(8,128)(2,1)S(1)}, bf16[256,576]{0,1:T(8,128)(2,1)}, u32[]{:S(2)}) copy-start(bf16[256,576]{0,1:T(8,128)(2,1)} %param.16) | copy-start | bytes 884740
  10.7 79.9 %all-to-all-start.2 = ((bf16[128,3,2304]{2,1,0:T(4,128)(2,1)}), bf16[128,3,2304]{2,1,0:T(4,128)(2,1)S(1)}, u32[]{:S(2)}, u32[]{:S(2)}) async-start(bf16[128,3,2304]{2,1,0:T(4,128)(2,1)} %reshape.378), calls=%async_computation.2 | async-start | bytes 4718592 | tf_op jit(solution)/shard_map/all_to_all | solution.py:91
  40.8 60.8 %copy-start.6 = (s32[128]{0:T(128)S(1)}, s32[128]{0:T(128)}, u32[]{:S(2)}) copy-start(s32[128]{0:T(128)} %param.23) | copy-start | bytes 1540
  90.6 1.4 copy-start.1
  92.1 82.8 %all-to-all-start.3 = ((bf16[128,18,432]{2,1,0:T(8,128)(2,1)}), bf16[128,18,432]{2,1,0:T(8,128)(2,1)S(1)}, u32[]{:S(2)}, u32[]{:S(2)}) async-start(bf16[128,18,432]{2,1,0:T(8,128)(2,1)} %reshape.380), calls=%async_computation.3 | async-start | bytes 6291456 | tf_op jit(solution)/shard_map/all_to_all | solution.py:129
  109.9 73.2 %copy-start.9 = (s32[128]{0:T(128)S(1)}, s32[128]{0:T(128)}, u32[]{:S(2)}) copy-start(s32[128]{0:T(128)} %param.24) | copy-start | bytes 1540
  174.9 65.0 %all-to-all-start = ((bf16[128,3,2304]{2,1,0:T(4,128)(2,1)}), bf16[128,3,2304]{2,1,0:T(4,128)(2,1)}, u32[]{:S(2)}, u32[]{:S(2)}) async-start(bf16[128,3,2304]{2,1,0:T(4,128)(2,1)} %reshape.373), calls=%async_computation | async-start | bytes 4718592 | tf_op jit(solution)/shard_map/all_to_all | solution.py:91
  239.8 82.6 %all-to-all-start.4 = ((bf16[128,18,432]{2,1,0:T(8,128)(2,1)}), bf16[128,18,432]{2,1,0:T(8,128)(2,1)S(1)}, u32[]{:S(2)}, u32[]{:S(2)}) async-start(bf16[128,18,432]{2,1,0:T(8,128)(2,1)} %gather_fusion.1), calls=%async_computation.4 | async-start | bytes 6291456 | tf_op jit(solution)/shard_map/all_to_all | solution.py:139
  264.4 65.9 %copy-start.7 = (s32[1,16]{1,0:T(1,128)S(1)}, s32[1,16]{1,0:T(1,128)}, u32[]{:S(2)}) copy-start(s32[1,16]{1,0:T(1,128)} %param.18) | copy-start | bytes 196
  264.4 66.1 %copy-start.4 = (bf16[2,8,576]{2,1,0:T(8,128)(2,1)S(1)}, bf16[2,8,576]{2,1,0:T(8,128)(2,1)}, u32[]{:S(2)}) copy-start(bf16[2,8,576]{2,1,0:T(8,128)(2,1)} %param.13) | copy-start | bytes 55300
  264.4 66.8 %copy-start.5 = (bf16[2,8,576]{2,1,0:T(8,128)(2,1)S(1)}, bf16[2,8,576]{2,1,0:T(8,128)(2,1)}, u32[]{:S(2)}) copy-start(bf16[2,8,576]{2,1,0:T(8,128)(2,1)} %param.14) | copy-start | bytes 55300
  264.4 68.1 %copy-start.8 = (f32[2,8,2]{1,2,0:T(2,128)S(1)}, f32[2,8,2]{1,2,0:T(2,128)}, u32[]{:S(2)}) copy-start(f32[2,8,2]{1,2,0:T(2,128)} %param.22) | copy-start | bytes 388
  322.5 62.6 %all-to-all-start.1 = ((bf16[128,3,2304]{2,1,0:T(4,128)(2,1)}), bf16[128,3,2304]{2,1,0:T(4,128)(2,1)}, u32[]{:S(2)}, u32[]{:S(2)}) async-start(bf16[128,3,2304]{2,1,0:T(4,128)(2,1)} %reshape.375), calls=%async_computation.1 | async-start | bytes 4718592 | tf_op jit(solution)/shard_map/all_to_all | solution.py:105
  340.3 3.1 copy-start.2
  385.1 72.0 %all-to-all-start.5 = ((bf16[128,3,2304]{2,1,0:T(4,128)(2,1)}), bf16[128,3,2304]{2,1,0:T(4,128)(2,1)}, u32[]{:S(2)}, u32[]{:S(2)}) async-start(bf16[128,3,2304]{2,1,0:T(4,128)(2,1)} %reshape.381), calls=%async_computation.5 | async-start | bytes 4718592 | tf_op jit(solution)/shard_map/all_to_all | solution.py:105
  392.8 12.3 %copy-start.3 = (bf16[2,8,2304]{2,1,0:T(8,128)(2,1)S(1)}, bf16[2,8,2304]{2,1,0:T(8,128)(2,1)}, u32[]{:S(2)}) copy-start(bf16[2,8,2304]{2,1,0:T(8,128)(2,1)} %param.19) | copy-start | bytes 221188
